TPU v7x, 32 devices: a whole 2x2x4 slice. The times are simulated.
32 devices in a mesh: gz: 8 (over z, x), gy: 4 (over y, core).
Axes of the slice: x: 2, y: 2, z: 4, core: 2. Of those that a mesh axis runs over, the one named last changes fastest.
Arguments:
- spectrum: float32 [3, 2, 4, 512, 4096], P(None, None, None, 'gy', 'gz'), may hold values from -6 to 6
- cells: int32 [2, 65536], P(None, ('gz', 'gy')), may hold values from 0 to 4095, as said below
- offsets: float32 [3, 65536], P(None, ('gz', 'gy')), may hold values from 0 to 1
- counts: int32 [32], P(('gz', 'gy')), may hold values from 1 to 2048, as said below
Outputs:
- coefficients: float32 [3, 4, 512, 4096], P(None, None, 'gy', 'gz')
- interpolated: float32 [3, 65536], P(None, ('gz', 'gy'))
Inputs may be any that keep to these rules, and one draw needn't show every extreme that they name: The particles of device number b = i * (size of gy) + j, at gz index i and gy index j, occupy slots b * 2048 to b * 2048 + 2047. Their base cells lie from two cells before that device's block to the cell just after its last one: along y from j * 128 - 2 to j * 128 + 128 modulo 512, along z from i * 512 - 2 to i * 512 + 512 modulo 4096. Empty slots hold such cells too. `counts`: live particles of each device fill its first slots; some device has exactly 2048.
All inputs are finite; a program needn't handle non-finite values.
Results may differ from a plain program's by a relative error of at most 0.000096.
Values sent between devices are 32-bit elements; how exact they have to be, the bound alone decides.
A program may use at most 128 MiB of HBM per device.

v0:
```python
import functools
import math

import jax
import jax.numpy as jnp
import numpy as np
from jax import lax
from jax.experimental import pallas as pl
from jax.experimental.pallas import tpu as pltpu
from jax.sharding import PartitionSpec as P

F32 = jnp.float32
BF16 = jnp.bfloat16


def split(value):
    high = value.astype(BF16)
    return high, (value - high.astype(F32)).astype(BF16)


def split_table(table):
    high = np.asarray(table, np.float32).astype(BF16)
    low = (table - high.astype(np.float64)).astype(np.float32).astype(BF16)
    return high, low


def dot(left, right):
    return jnp.dot(left, right, preferred_element_type=F32)


def dft(items):
    count = len(items)
    if count == 1:
        return items
    even = dft(items[0::2])
    odd = dft(items[1::2])
    half = count // 2
    low, high = [], []
    for m in range(half):
        er, ei = even[m]
        xr, xi = odd[m]
        if m == 0:
            tr, ti = xr, xi
        elif 4 * m == count:
            tr, ti = -xi, xr
        elif 8 * m == count:
            s = math.sqrt(0.5)
            tr, ti = (xr - xi) * s, (xr + xi) * s
        elif 8 * m == 3 * count:
            s = math.sqrt(0.5)
            tr, ti = (xr + xi) * -s, (xr - xi) * s
        else:
            c, s = math.cos(2 * math.pi * m / count), math.sin(2 * math.pi * m / count)
            tr, ti = xr * c - xi * s, xr * s + xi * c
        low.append((er + tr, ei + ti))
        high.append((er - tr, ei - ti))
    return low + high


def line_kernel(re_ref, im_ref, factor_ref, tcos_ref, tsin_ref, whi_ref, wlo_ref, perm_ref,
                out_ref, yhi_ref, ylo_ref, z_ref):
    parts, lines, width = re_ref.shape
    step = 16

    @pl.loop(0, lines // step)
    def _(group):
        rows = pl.ds(pl.multiple_of(group * step, step), step)
        for tile in range(width // 128):
            lanes = slice(tile * 128, tile * 128 + 128)
            items = []
            for i in range(parts):
                f = factor_ref[i : i + 1, lanes]
                items.append((re_ref[i, rows, lanes] * f, im_ref[i, rows, lanes] * f))
            for m, (yr, yi) in enumerate(dft(items)):
                c, s = tcos_ref[m : m + 1, lanes], tsin_ref[m : m + 1, lanes]
                zr, zi = yr * c - yi * s, yr * s + yi * c
                shifted = slice(width + tile * 128, width + tile * 128 + 128)
                hi, lo = split(zr)
                yhi_ref[m, rows, lanes] = hi
                ylo_ref[m, rows, lanes] = lo
                hi, lo = split(zi)
                yhi_ref[m, rows, shifted] = hi
                ylo_ref[m, rows, shifted] = lo

    @pl.loop(0, parts)
    def _(m):
        yhi = yhi_ref[m]
        z_ref[m] = dot(yhi, whi_ref[...]) + dot(ylo_ref[m], whi_ref[...]) + dot(yhi, wlo_ref[...])

    each = width // parts
    for target in range(parts):
        lanes = slice(target * each, target * each + each)
        joined = jnp.concatenate([z_ref[m, :, lanes] for m in range(parts)], axis=1)
        hi, lo = split(joined)
        out_ref[target] = dot(hi, perm_ref[...]) + dot(lo, perm_ref[...])


def transform(real, imag, tables):
    parts, lines, width = real.shape
    return pl.pallas_call(
        line_kernel,
        out_shape=jax.ShapeDtypeStruct((parts, lines, width), F32),
        in_specs=[pl.BlockSpec(memory_space=pltpu.VMEM)] * 8,
        out_specs=pl.BlockSpec(memory_space=pltpu.VMEM),
        scratch_shapes=[
            pltpu.VMEM((parts, lines, 2 * width), BF16),
            pltpu.VMEM((parts, lines, 2 * width), BF16),
            pltpu.VMEM((parts, lines, width), F32),
        ],
        compiler_params=pltpu.CompilerParams(vmem_limit_bytes=24 << 20),
        cost_estimate=pl.CostEstimate(
            flops=20 * parts * lines * width * width, bytes_accessed=12 * parts * lines * width,
            transcendentals=0),
    )(real, imag, *tables)


def line_tables(parts, width):
    length = parts * width
    k = np.arange(length, dtype=np.float64)
    symbol = (4.0 + 2.0 * np.cos(k * (2.0 * math.pi / length))) / 6.0
    factor = (1.0 / (symbol * math.sqrt(length))).reshape(parts, width).astype(np.float32)
    turn = np.outer(np.arange(parts), np.arange(width)) * (2.0 * math.pi / length)
    angle = (np.outer(np.arange(width), np.arange(width)) % width) * (2.0 * math.pi / width)
    whi, wlo = split_table(np.concatenate([np.cos(angle), -np.sin(angle)], axis=0))
    each = width // parts
    perm = np.zeros((width, width), np.float32)
    for m in range(parts):
        for q in range(each):
            perm[m * each + q, parts * q + m] = 1.0
    made = (factor, np.cos(turn).astype(np.float32), np.sin(turn).astype(np.float32),
            whi, wlo, perm.astype(BF16))
    return made


MESH = pl.DeviceIdType.MESH


SUB = 2


def hub_kernel(spec, count_ref, cells, offs, factor, tcos, tsin, whi, wlo, perm, out, vals,
               xbuf, yhi, ylo, zown, zsend, zrecv, total, field, edge_z, halo_z, halo_y, corner,
               fhi, flo, pzhi, pzlo, py,
               send_a, recv_a, cross_s, cross_r, dist_s, dist_r, loc, keep,
               ez_s, ez_r, ey_s, ey_r, ec_s, ec_r, out_s):
    components, _, planes, rows_y, width = spec.shape
    lines = rows_y // (2 * SUB)
    chunks = components * planes * SUB
    per_part = planes * SUB
    slots = cells.shape[1]
    chunk = 256
    groups = slots // chunk
    parts = 8
    each = width // parts
    wide = width // 2
    me = lax.axis_index("gz")
    half = me // 4
    side = me % 2
    is_hub = ((me // 2) == 1) | ((me // 2) == 2)
    hub_same = 2 + 2 * half + side
    hub_other = 2 + 2 * half + (1 - side)
    leaf_same = 6 * half + side
    leaf_other = 6 * half + (1 - side)
    partner = 4 - 2 * half + side
    z_next, z_prev = lax.rem(me + 1, 8), lax.rem(me + 7, 8)
    gy, gy_count = lax.axis_index("gy"), lax.axis_size("gy")
    y_next, y_prev = lax.rem(gy + 1, gy_count), lax.rem(gy + gy_count - 1, gy_count)

    barrier = pltpu.get_barrier_semaphore()

    def greet(peer):
        pl.semaphore_signal(barrier, inc=1, device_id={"gz": peer}, device_id_type=MESH)

    def greet_ring():
        greet(z_next)
        greet(z_prev)
        for peer in (y_next, y_prev):
            pl.semaphore_signal(barrier, inc=1, device_id={"gy": peer}, device_id_type=MESH)

    @pl.when(is_hub)
    def _():
        greet_ring()
        greet(leaf_same)
        greet(leaf_other)
        greet(hub_other)
        greet(partner)
        pl.semaphore_wait(barrier, 8)

    @pl.when(jnp.logical_not(is_hub))
    def _():
        greet_ring()
        greet(hub_same)
        greet(hub_other)
        pl.semaphore_wait(barrier, 6)

    def rows_of(j, which):
        return pl.ds(pl.multiple_of(which * (lines * SUB) + (j % SUB) * lines, lines), lines)

    def remote(source, target, send, recv, peer, axis="gz"):
        return pltpu.make_async_remote_copy(
            src_ref=source, dst_ref=target, send_sem=send, recv_sem=recv,
            device_id={axis: peer}, device_id_type=MESH)

    def source(j, which):
        return spec.at[j // per_part, :, (j // SUB) % planes, rows_of(j, which), :]

    def give(j, which, n, peer):
        return remote(source(j, which),
                      xbuf.at[j, me % 4], send_a.at[j, n], recv_a.at[j, me % 4], peer)

    def arrival(j, slot):
        return remote(xbuf.at[j, slot], xbuf.at[j, slot], send_a.at[j, 0], recv_a.at[j, slot],
                      partner)

    def own(j):
        return pltpu.make_async_copy(source(j, side),
                                     xbuf.at[j, me % 4], loc.at[j])

    def cross(j):
        return remote(zsend.at[j], zrecv.at[j], cross_s.at[j], cross_r.at[j], partner)

    def place(j, which):
        return field.at[j // SUB, rows_of(j, which), :]

    def hand(j, n, peer):
        return remote(total.at[j, peer % 4], place(j, side), dist_s.at[j, n],
                      dist_r.at[j, side], peer)

    def taken(j, which):
        return remote(total.at[j, 0], place(j, which), dist_s.at[j, 0], dist_r.at[j, which],
                      hub_other)

    def kept(j):
        return pltpu.make_async_copy(total.at[j, me % 4], place(j, side), keep.at[j])

    def planes_of(c):
        return pl.ds(c * planes, planes)

    def edge_copies(c):
        return (
            remote(edge_z.at[c, 0], halo_z.at[c, 0], ez_s.at[c, 0], ez_r.at[c, 0], z_next),
            remote(edge_z.at[c, 1], halo_z.at[c, 1], ez_s.at[c, 1], ez_r.at[c, 1], z_prev),
            remote(field.at[planes_of(c), rows_y - 8 :, :], halo_y.at[c, 0], ey_s.at[c, 0],
                   ey_r.at[c, 0], y_next, "gy"),
            remote(field.at[planes_of(c), 0:8, :], halo_y.at[c, 1], ey_s.at[c, 1],
                   ey_r.at[c, 1], y_prev, "gy"),
        )

    def corner_copies(c):
        return (
            remote(halo_z.at[c], corner.at[c, 0], ec_s.at[c, 0], ec_r.at[c, 0], y_next, "gy"),
            remote(halo_z.at[c], corner.at[c, 1], ec_s.at[c, 1], ec_r.at[c, 1], y_prev, "gy"),
        )

    def out_copy(c):
        return pltpu.make_async_copy(field.at[planes_of(c)], out.at[c], out_s.at[c])

    def send_edges(c):
        @pl.loop(0, planes)
        def _(x):
            at = pl.ds(pl.multiple_of(x * 8, 8), 8)
            tail = field[c * planes + x, :, width - 128 :]
            edge_z[c, 0, at, :] = jnp.transpose(tail)[120:128]
            edge_z[c, 1, at, :] = jnp.transpose(field[c * planes + x, :, 0:128])[0:8]
        for copy in edge_copies(c):
            copy.start()
        out_copy(c).start()

    def send_corners(c):
        first, second, _, _ = edge_copies(c)
        first.wait_recv()
        second.wait_recv()
        for copy in corner_copies(c):
            copy.start()

    def prepare(c):
        _, _, third, fourth = edge_copies(c)
        third.wait_recv()
        fourth.wait_recv()
        for copy in corner_copies(c):
            copy.wait_recv()
        none = jnp.zeros((112, 128), F32)

        @pl.loop(0, planes)
        def _(x):
            at = pl.ds(pl.multiple_of(x * 8, 8), 8)
            main = pl.ds(pl.multiple_of(x * rows_y, rows_y), rows_y)
            edge = pl.ds(pl.multiple_of(planes * rows_y + x * 16, 16), 16)

            def unfold(low, high):
                return jnp.transpose(jnp.concatenate([low, high, none], axis=0))

            fhi[main, 0:width], flo[main, 0:width] = split(field[c * planes + x])
            fhi[main, width:], flo[main, width:] = split(
                unfold(halo_z[c, 0, at, :], halo_z[c, 1, at, :]))
            fhi[edge, 0:width], flo[edge, 0:width] = split(
                jnp.concatenate([halo_y[c, 0, x], halo_y[c, 1, x]], axis=0))
            low = unfold(corner[c, 0, 0, at, :], corner[c, 0, 1, at, :])[rows_y - 8 :]
            high = unfold(corner[c, 1, 0, at, :], corner[c, 1, 1, at, :])[0:8]
            fhi[edge, width:], flo[edge, width:] = split(jnp.concatenate([low, high], axis=0))

    def lanes_of(u):
        return pl.ds(pl.multiple_of(u * chunk, chunk), chunk)

    def first_cell(row, start, length, at):
        near = cells[row : row + 1, at] - (start - 2)
        near = jnp.where(near < 0, near + length, near)
        return jnp.where(near >= length, near - length, near) - 3

    def weigh(u):
        at = lanes_of(u)
        wy = spline_weights(offs[1:2, at])
        wz = spline_weights(offs[2:3, at])
        first_y = first_cell(0, gy * rows_y, gy_count * rows_y, at)
        first_z = first_cell(1, me * width, 8 * width, at)

        @pl.loop(0, width // 32)
        def _(tile):
            spot = lax.broadcasted_iota(jnp.int32, (32, chunk), 0) + tile * 32
            rows = pl.ds(pl.multiple_of(tile * 32, 32), 32)
            pzhi[rows, at], pzlo[rows, at] = split(dense(spot - first_z, wz))
        h = lax.broadcasted_iota(jnp.int32, (16, chunk), 0)
        spot = jnp.where(h < 8, h - 8, h + (width - 8))
        pzhi[width : width + 16, at], pzlo[width : width + 16, at] = split(
            dense(spot - first_z, wz))
        zero = jnp.zeros((112, chunk), BF16)
        pzhi[width + 16 :, at] = zero
        pzlo[width + 16 :, at] = zero

        @pl.loop(0, (rows_y + 16) // 16)
        def _(tile):
            spot = lax.broadcasted_iota(jnp.int32, (16, chunk), 0) + (tile * 16 - 8)
            rows = pl.ds(pl.multiple_of(tile * 16, 16), 16)
            py[rows, at] = dense(spot - first_y, wy)

    def interpolate(c, u):
        at = lanes_of(u)
        wx = spline_weights(offs[0:1, at])
        high = fhi[...]
        field_z = (dot(high, pzhi[:, at]) + dot(flo[...], pzhi[:, at]) + dot(high, pzlo[:, at]))
        value = jnp.zeros((1, chunk), F32)
        for x in range(planes):
            begin = planes * rows_y + x * 16
            part = jnp.sum(field_z[x * rows_y : (x + 1) * rows_y] * py[8 : 8 + rows_y, at],
                           axis=0, keepdims=True)
            ends = (field_z[begin : begin + 8] * py[0:8, at]
                    + field_z[begin + 8 : begin + 16] * py[8 + rows_y :, at])
            value = value + (part + jnp.sum(ends, axis=0, keepdims=True)) * wx[x]
        slot = lax.broadcasted_iota(jnp.int32, (1, chunk), 1) + u * chunk
        vals[c, :, at] = jnp.where(slot < count_ref[0], value, 0.0)

    def finish():
        @pl.loop(0, components)
        def _(c):
            for copy in edge_copies(c) + corner_copies(c):
                copy.wait_send()
            out_copy(c).wait()

    @pl.when(jnp.logical_not(is_hub))
    def _():
        @pl.loop(0, chunks)
        def _(j):
            give(j, side, 0, hub_same).start()
            give(j, 1 - side, 1, hub_other).start()

        pl.loop(0, groups)(weigh)

        @pl.loop(0, components)
        def _(c):
            @pl.loop(0, per_part)
            def _(n):
                taken(c * per_part + n, side).wait_recv()
                taken(c * per_part + n, 1 - side).wait_recv()
            send_edges(c)
            send_corners(c)
            prepare(c)

            @pl.loop(0, groups)
            def _(u):
                interpolate(c, u)

        @pl.loop(0, chunks)
        def _(j):
            give(j, side, 0, hub_same).wait_send()
            give(j, 1 - side, 1, hub_other).wait_send()
        finish()

    def first_stage(j):
        own(j).wait()
        arrival(j, leaf_same % 4).wait_recv()
        arrival(j, leaf_other % 4).wait_recv()
        arrival(j, hub_other % 4).wait_recv()
        root = math.sqrt(0.5)

        @pl.loop(0, lines // 16)
        def _(group):
            rows = pl.ds(pl.multiple_of(group * 16, 16), 16)
            for tile in range(width // 128):
                lanes = slice(tile * 128, tile * 128 + 128)
                items = []
                for i in range(4):
                    f = factor[half, i : i + 1, lanes]
                    items.append((xbuf[j, i, 0, rows, lanes] * f, xbuf[j, i, 1, rows, lanes] * f))
                (ar, ai), (br, bi), (cr, ci), (dr, di) = items
                turned = [(ar, ai), ((br - bi) * root, (br + bi) * root), (-ci, cr),
                          ((dr + di) * -root, (dr - di) * root)]
                even, odd = dft(items), dft(turned)
                for m in range(parts):
                    yr, yi = (odd if m % 2 else even)[m // 2]
                    c, s = tcos[half, m : m + 1, lanes], tsin[half, m : m + 1, lanes]
                    zr, zi = yr * c - yi * s, yr * s + yi * c
                    at = pl.ds(pl.multiple_of(m * lines + group * 16, 16), 16)
                    shifted = slice(width + tile * 128, width + tile * 128 + 128)
                    hi, lo = split(zr)
                    yhi[at, lanes] = hi
                    ylo[at, lanes] = lo
                    hi, lo = split(zi)
                    yhi[at, shifted] = hi
                    ylo[at, shifted] = lo

        def product(which):
            lanes = pl.ds(pl.multiple_of(which * wide, wide), wide)
            left = yhi[...]
            return dot(left, whi[:, lanes]) + dot(ylo[...], whi[:, lanes]) + dot(left, wlo[:, lanes])

        zsend[j] = product(1 - half)
        cross(j).start()
        zown[j % 2] = product(half)

    def second_stage(j):
        cross(j).wait_recv()
        for target in range(4):
            lanes = slice(target * each, target * each + each)
            pieces = []
            for m in range(parts):
                rows = slice(m * lines, m * lines + lines)
                pieces.append(zown[j % 2, rows, lanes] + zrecv[j, rows, lanes])
            hi, lo = split(jnp.concatenate(pieces, axis=1))
            total[j, target] = dot(hi, perm[...]) + dot(lo, perm[...])
        hand(j, 0, leaf_same).start()
        hand(j, 1, leaf_other).start()
        hand(j, 2, hub_other).start()
        kept(j).start()

    @pl.when(is_hub)
    def _():
        @pl.loop(0, chunks)
        def _(j):
            own(j).start()
            give(j, 1 - side, 0, hub_other).start()

        @pl.loop(0, chunks + 1)
        def _(t):
            @pl.when(t < chunks)
            def _():
                first_stage(t)

            @pl.when(t > 0)
            def _():
                second_stage(t - 1)

            @pl.when(t < groups)
            def _():
                weigh(t)

        @pl.loop(0, components)
        def _(c):
            @pl.loop(0, per_part)
            def _(n):
                kept(c * per_part + n).wait()
                taken(c * per_part + n, 1 - side).wait_recv()
            send_edges(c)

        @pl.loop(0, components)
        def _(c):
            send_corners(c)

        @pl.loop(0, components)
        def _(c):
            prepare(c)

            @pl.loop(0, groups)
            def _(u):
                interpolate(c, u)

        @pl.loop(0, chunks)
        def _(j):
            give(j, 1 - side, 0, hub_other).wait_send()
            cross(j).wait_send()
            hand(j, 0, leaf_same).wait_send()
            hand(j, 1, leaf_other).wait_send()
            hand(j, 2, hub_other).wait_send()
        finish()


def hub_program(spectrum, cells, offsets, counts, tables):
    components, _, planes, rows_y, width = spectrum.shape
    slots = cells.shape[1]
    lines = rows_y // (2 * SUB)
    chunks = components * planes * SUB
    factor, tcos, tsin, whi, wlo, perm = tables
    sign = np.ones((2, 8, 1), np.float32)
    sign[1, 1::2] = -1.0
    factor = factor.reshape(2, 4, width)
    tcos, tsin = tcos[None] * sign, tsin[None] * sign
    dma = pltpu.SemaphoreType.DMA
    vmem = pl.BlockSpec(memory_space=pltpu.VMEM)
    body = planes * (rows_y + 16)
    out, values = pl.pallas_call(
        hub_kernel,
        out_shape=(jax.ShapeDtypeStruct((components, planes, rows_y, width), F32),
                   jax.ShapeDtypeStruct((components, 1, slots), F32)),
        in_specs=[pl.BlockSpec(memory_space=pl.ANY), pl.BlockSpec(memory_space=pltpu.SMEM)]
        + [vmem] * 8,
        out_specs=(pl.BlockSpec(memory_space=pl.ANY), vmem),
        scratch_shapes=[
            pltpu.VMEM((chunks, 4, 2, lines, width), F32),
            pltpu.VMEM((8 * lines, 2 * width), BF16),
            pltpu.VMEM((8 * lines, 2 * width), BF16),
            pltpu.VMEM((2, 8 * lines, width // 2), F32),
            pltpu.VMEM((chunks, 8 * lines, width // 2), F32),
            pltpu.VMEM((chunks, 8 * lines, width // 2), F32),
            pltpu.VMEM((chunks, 4, lines, width), F32),
            pltpu.VMEM((components * planes, rows_y, width), F32),
            pltpu.VMEM((components, 2, planes * 8, 128), F32),
            pltpu.VMEM((components, 2, planes * 8, 128), F32),
            pltpu.VMEM((components, 2, planes, 8, width), F32),
            pltpu.VMEM((components, 2, 2, planes * 8, 128), F32),
            pltpu.VMEM((body, width + 128), BF16),
            pltpu.VMEM((body, width + 128), BF16),
            pltpu.VMEM((width + 128, slots), BF16),
            pltpu.VMEM((width + 128, slots), BF16),
            pltpu.VMEM((rows_y + 16, slots), F32),
            dma((chunks, 2)),
            dma((chunks, 4)),
            dma((chunks,)),
            dma((chunks,)),
            dma((chunks, 3)),
            dma((chunks, 2)),
            dma((chunks,)),
            dma((chunks,)),
        ] + [dma((components, 2))] * 6 + [dma((components,))],
        compiler_params=pltpu.CompilerParams(
            collective_id=0, has_side_effects=True, vmem_limit_bytes=63 << 20),
    )(spectrum, counts, cells, offsets, factor, tcos, tsin, whi, wlo, perm)
    return out, values.reshape(components, slots)


def general_transform(real, imag):
    parts, lines, width = real.shape
    length = parts * width
    k = np.arange(length, dtype=np.float64)
    symbol = (4.0 + 2.0 * np.cos(k * (2.0 * math.pi / length))) / 6.0
    factor = (1.0 / (symbol * math.sqrt(length))).reshape(parts, 1, width).astype(np.float32)
    real, imag = real * factor, imag * factor
    highest = lax.Precision.HIGHEST

    def table(left, right, modulus):
        angle = (np.outer(np.arange(left), np.arange(right)) % modulus) * (2 * math.pi / modulus)
        return np.cos(angle).astype(np.float32), np.sin(angle).astype(np.float32)

    c, s = table(parts, parts, parts)
    first = functools.partial(jnp.einsum, "ilk,im->mlk", precision=highest)
    yr, yi = first(real, c) - first(imag, s), first(real, s) + first(imag, c)
    c, s = table(parts, width, length)
    c, s = c[:, None], s[:, None]
    zr, zi = yr * c - yi * s, yr * s + yi * c
    c, s = table(width, width, width)
    last = functools.partial(jnp.einsum, "mlk,kq->lqm", precision=highest)
    out = (last(zr, c) - last(zi, s)).reshape(lines, parts, width)
    return jnp.moveaxis(out, 1, 0)


def spline_weights(frac):
    cube = frac * frac * frac
    square = frac * frac
    first = (1.0 - frac) * (1.0 - frac) * (1.0 - frac) / 6.0
    second = (3.0 * cube - 6.0 * square + 4.0) / 6.0
    third = (-3.0 * cube + 3.0 * square + 3.0 * frac + 1.0) / 6.0
    fourth = cube / 6.0
    return [first, second, third, fourth]


def dense(distance, weights):
    total = jnp.zeros(distance.shape, F32)
    for tap in range(4):
        total = jnp.where(distance == tap, weights[tap], total)
    return total


def halo_place(rows, size, chunk):
    h = lax.broadcasted_iota(jnp.int32, (rows, chunk), 0)
    return jnp.where(h < 3, h - 3, jnp.where(h < 6, h + (size - 3), -1000000))


def point_kernel(planes, count_ref, near_ref, off_ref, main_ref, zh_ref, yh_ref, cor_ref,
                 out_ref, fhi, flo, whi, wlo, wy_ref):
    block, width = main_ref.shape[0] // 3, main_ref.shape[1]
    rows_y = block // planes
    chunk = near_ref.shape[1]
    body = 3 * block

    @pl.when(pl.program_id(0) == 0)
    def _():
        for c in range(3):
            @pl.loop(0, planes)
            def _(x):
                dst = pl.ds(pl.multiple_of(c * block + x * rows_y, rows_y), rows_y)
                hi, lo = split(main_ref[dst, :])
                fhi[dst, 0:width] = hi
                flo[dst, 0:width] = lo
                hi, lo = split(zh_ref[dst, :])
                fhi[dst, width:] = hi
                flo[dst, width:] = lo
        hi, lo = split(yh_ref[...])
        fhi[body:, 0:width] = hi
        flo[body:, 0:width] = lo
        hi, lo = split(cor_ref[...])
        fhi[body:, width:] = hi
        flo[body:, width:] = lo

    wx = spline_weights(off_ref[0:1, :])
    wy = spline_weights(off_ref[1:2, :])
    wz = spline_weights(off_ref[2:3, :])
    first_y = near_ref[0:1, :] - 1
    first_z = near_ref[1:2, :] - 1
    for tile in range(width // 128):
        place = lax.broadcasted_iota(jnp.int32, (128, chunk), 0) + tile * 128
        hi, lo = split(dense(place - first_z, wz))
        whi[tile * 128 : tile * 128 + 128, :] = hi
        wlo[tile * 128 : tile * 128 + 128, :] = lo
    hi, lo = split(dense(halo_place(128, width, chunk) - first_z, wz))
    whi[width:, :] = hi
    wlo[width:, :] = lo
    place = lax.broadcasted_iota(jnp.int32, (rows_y, chunk), 0)
    wy_ref[0:rows_y, :] = dense(place - first_y, wy)
    wy_ref[rows_y:, :] = dense(halo_place(8, rows_y, chunk) - first_y, wy)

    def layer(begin, rows):
        high = fhi[begin : begin + rows, :]
        return (dot(high, whi[...]) + dot(flo[begin : begin + rows, :], whi[...])
                + dot(high, wlo[...]))

    slot = lax.broadcasted_iota(jnp.int32, (1, chunk), 1) + pl.program_id(0) * chunk
    live = slot < count_ref[0]
    edge = layer(body, 3 * planes * 8)
    for c in range(3):
        inner = layer(c * block, block)
        value = jnp.zeros((1, chunk), F32)
        for x in range(planes):
            part = jnp.sum(inner[x * rows_y : (x + 1) * rows_y] * wy_ref[0:rows_y, :], axis=0,
                           keepdims=True)
            at = (c * planes + x) * 8
            part = part + jnp.sum(edge[at : at + 8] * wy_ref[rows_y:, :], axis=0, keepdims=True)
            value = value + part * wx[x]
        out_ref[c : c + 1, :] = jnp.where(live, value, 0.0)


def sample(counts, near, offsets, main, zh, yh, cor, planes):
    slots = near.shape[1]
    block, width = main.shape[0] // 3, main.shape[1]
    rows_y = block // planes
    chunk = math.gcd(slots, 256)
    whole = pl.BlockSpec(memory_space=pltpu.VMEM)
    return pl.pallas_call(
        functools.partial(point_kernel, planes),
        out_shape=jax.ShapeDtypeStruct((3, slots), F32),
        grid=(slots // chunk,),
        in_specs=[
            pl.BlockSpec(memory_space=pltpu.SMEM),
            pl.BlockSpec((2, chunk), lambda i: (0, i)),
            pl.BlockSpec((3, chunk), lambda i: (0, i)),
        ] + [whole] * 4,
        out_specs=pl.BlockSpec((3, chunk), lambda i: (0, i)),
        scratch_shapes=[
            pltpu.VMEM((3 * block + 24 * planes, width + 128), BF16),
            pltpu.VMEM((3 * block + 24 * planes, width + 128), BF16),
            pltpu.VMEM((width + 128, chunk), BF16),
            pltpu.VMEM((width + 128, chunk), BF16),
            pltpu.VMEM((rows_y + 8, chunk), F32),
        ],
        compiler_params=pltpu.CompilerParams(vmem_limit_bytes=32 << 20),
    )(counts, near, offsets, main, zh, yh, cor)


def ring(axis):
    count = lax.axis_size(axis)
    forward = [(i, (i + 1) % count) for i in range(count)]
    return forward, [(b, a) for a, b in forward]


def per_device(spectrum, cells, offsets, counts):
    components, halves, planes, rows_y, rows_z = spectrum.shape
    parts = lax.axis_size("gz")
    length_z = rows_z * parts
    length_y = rows_y * lax.axis_size("gy")
    z_start = lax.axis_index("gz") * rows_z
    y_start = lax.axis_index("gy") * rows_y
    lines = planes * rows_y // parts
    tiled = rows_z % (parts * 64) == 0 and lines % 16 == 0
    tables = line_tables(parts, rows_z) if tiled else None
    exchange = functools.partial(
        lax.all_to_all, axis_name="gz", split_axis=0, concat_axis=0, tiled=True)
    if (parts == 8 and tiled and rows_y == 128 and cells.shape[1] % 256 == 0
            and cells.shape[1] // 256 <= components * planes * SUB):
        return hub_program(spectrum, cells, offsets, counts, tables)
    blocks = []
    for c in range(components):
        real = exchange(spectrum[c, 0].reshape(parts, lines, rows_z))
        imag = exchange(spectrum[c, 1].reshape(parts, lines, rows_z))
        done = transform(real, imag, tables) if tiled else general_transform(real, imag)
        blocks.append(exchange(done).reshape(planes, rows_y, rows_z))
    coefficients = jnp.stack(blocks)
    pieces = components * planes
    field = coefficients.reshape(pieces, rows_y, rows_z)

    forward, backward = ring("gz")
    flat_low = jnp.swapaxes(field[:, :, rows_z - 3 :], 1, 2)
    flat_high = jnp.swapaxes(field[:, :, :3], 1, 2)
    z_halo = jnp.concatenate(
        [lax.ppermute(flat_low, "gz", forward), lax.ppermute(flat_high, "gz", backward)], axis=1)
    forward, backward = ring("gy")
    y_low = lax.ppermute(field[:, rows_y - 3 :], "gy", forward)
    y_high = lax.ppermute(field[:, :3], "gy", backward)
    c_low = lax.ppermute(z_halo[:, :, rows_y - 3 :], "gy", forward)
    c_high = lax.ppermute(z_halo[:, :, :3], "gy", backward)
    y_halo = jnp.concatenate([y_low, y_high, jnp.zeros((pieces, 2, rows_z), F32)], axis=1)
    corner = jnp.concatenate([c_low, c_high, jnp.zeros((pieces, 6, 2), F32)], axis=2)

    def wide(item):
        item = jnp.swapaxes(item, 1, 2)
        return jnp.pad(item, ((0, 0), (0, 0), (0, 122))).reshape(-1, 128)

    near_y = (cells[0] - y_start + 2) % length_y - 2
    near_z = (cells[1] - z_start + 2) % length_z - 2
    interpolated = sample(
        counts, jnp.stack([near_y, near_z]), offsets,
        field.reshape(pieces * rows_y, rows_z),
        wide(z_halo), y_halo.reshape(pieces * 8, rows_z), wide(corner), planes)
    return (coefficients, interpolated)


def solution(mesh):
    placed = (
        P(None, None, None, "gy", "gz"),
        P(None, ("gz", "gy")),
        P(None, ("gz", "gy")),
        P(("gz", "gy")),
    )
    return jax.shard_map(
        per_device,
        mesh=mesh,
        in_specs=placed,
        out_specs=(P(None, None, "gy", "gz"), P(None, ("gz", "gy"))),
        check_vma=False,
    )
```

profile of v0, /device:TPU:8, one launch (start us, length us, event | category | flops | bytes accessed | tf_op | source)
XLA Modules:
  0.0 216.3 jit_solution(14909189035873887923)
XLA Ops:
  1.3 209.8 %shard_map.113 = (f32[3,4,128,512]{3,2,1,0:T(8,128)}, f32[3,1,2048]{2,1,0:T(1,128)}) custom-call(f32[3,2,4,128,512]{4,3,2,1,0:T(8,128)} %spec.1, s32[1]{0:T(128)S(6)} %copy.16.count_ref, s32[2,2048]{1,0:T(2,128)} %cells.1, f32[3,2048]{1,0:T(4,128)} %offs.1, f32[2,4,512]{2,1,0:T(4,128)} %constant.12.clone.factor, f32[2,8,512]{2,1,0:T(8,128)} %constant.13.clone.tcos, ...), custom_call_target="tpu_custom_call" | custom-call | tf_op jit(solution)/shard_map/pallas_call | solution.py:509
  211.1 1.4 copy.14
  212.5 3.9 %copy.17 = f32[3,4,128,512]{3,2,1,0:T(8,128)} copy(f32[3,4,128,512]{3,2,1,0:T(8,128)} %get-tuple-element.8) | data formatting | bytes 6291456
where the time goes:
time: 217 us; the launch traced here: 216 us
  Pallas kernels  210 us (97%)
  local copies, waits for them, and re-layouts  5.22 us (2%)
    pallas_call x1, Pallas kernels, hub_program(): pl.pallas_call(hub_kernel, out_shape=(jax.ShapeDtypeStruct((components, p...  210 us
    unnamed x2, local copies, waits for them, and re-layouts  5.22 us

commit v1 on v0

--- a/solution.py
+++ b/solution.py
@@ -135,24 +135,31 @@
 MESH = pl.DeviceIdType.MESH
 
 
-SUB = 2
+SUB = 4
+DIRECT = 6
+AHEAD = 6
+LAG = 2
+FIRST_RELAYS = 16
+RELAYS = 6
 
 
 def hub_kernel(spec, count_ref, cells, offs, factor, tcos, tsin, whi, wlo, perm, out, vals,
                xbuf, yhi, ylo, zown, zsend, zrecv, total, field, edge_z, halo_z, halo_y, corner,
-               fhi, flo, pzhi, pzlo, py,
+               fboth, pzhi, pzlo, py, wxs,
                send_a, recv_a, cross_s, cross_r, dist_s, dist_r, loc, keep,
                ez_s, ez_r, ey_s, ey_r, ec_s, ec_r, out_s):
     components, _, planes, rows_y, width = spec.shape
     lines = rows_y // (2 * SUB)
-    chunks = components * planes * SUB
-    per_part = planes * SUB
+    pieces = components * planes
+    chunks = pieces * SUB
     slots = cells.shape[1]
     chunk = 256
     groups = slots // chunk
+    share = groups // SUB
     parts = 8
     each = width // parts
     wide = width // 2
+    body = rows_y + 16
     me = lax.axis_index("gz")
     half = me // 4
     side = me % 2
@@ -165,49 +172,47 @@
     z_next, z_prev = lax.rem(me + 1, 8), lax.rem(me + 7, 8)
     gy, gy_count = lax.axis_index("gy"), lax.axis_size("gy")
     y_next, y_prev = lax.rem(gy + 1, gy_count), lax.rem(gy + gy_count - 1, gy_count)
+    diagonals = [{"gz": z, "gy": y} for z in (z_next, z_prev) for y in (y_next, y_prev)]
 
     barrier = pltpu.get_barrier_semaphore()
 
     def greet(peer):
-        pl.semaphore_signal(barrier, inc=1, device_id={"gz": peer}, device_id_type=MESH)
-
-    def greet_ring():
-        greet(z_next)
-        greet(z_prev)
-        for peer in (y_next, y_prev):
-            pl.semaphore_signal(barrier, inc=1, device_id={"gy": peer}, device_id_type=MESH)
+        pl.semaphore_signal(barrier, inc=1, device_id=peer, device_id_type=MESH)
+
+    for peer in [{"gz": z_next}, {"gz": z_prev}, {"gy": y_next}, {"gy": y_prev}] + diagonals:
+        greet(peer)
 
     @pl.when(is_hub)
     def _():
-        greet_ring()
-        greet(leaf_same)
-        greet(leaf_other)
-        greet(hub_other)
-        greet(partner)
-        pl.semaphore_wait(barrier, 8)
+        for peer in (leaf_same, leaf_other, hub_other, partner):
+            greet({"gz": peer})
 
     @pl.when(jnp.logical_not(is_hub))
     def _():
-        greet_ring()
-        greet(hub_same)
-        greet(hub_other)
-        pl.semaphore_wait(barrier, 6)
+        for peer in (hub_same, hub_other, leaf_other):
+            greet({"gz": peer})
 
     def rows_of(j, which):
         return pl.ds(pl.multiple_of(which * (lines * SUB) + (j % SUB) * lines, lines), lines)
 
-    def remote(source, target, send, recv, peer, axis="gz"):
+    def remote(source, target, send, recv, peer):
         return pltpu.make_async_remote_copy(
             src_ref=source, dst_ref=target, send_sem=send, recv_sem=recv,
-            device_id={axis: peer}, device_id_type=MESH)
+            device_id=peer if isinstance(peer, dict) else {"gz": peer}, device_id_type=MESH)
 
     def source(j, which):
-        return spec.at[j // per_part, :, (j // SUB) % planes, rows_of(j, which), :]
+        piece = j // SUB
+        return spec.at[piece // planes, :, piece % planes, rows_of(j, which), :]
 
     def give(j, which, n, peer):
         return remote(source(j, which),
                       xbuf.at[j, me % 4], send_a.at[j, n], recv_a.at[j, me % 4], peer)
 
+    def relay(j):
+        slot = leaf_other % 4
+        return remote(xbuf.at[j, slot], xbuf.at[j, slot], send_a.at[j, 2], recv_a.at[j, slot],
+                      hub_same)
+
     def arrival(j, slot):
         return remote(xbuf.at[j, slot], xbuf.at[j, slot], send_a.at[j, 0], recv_a.at[j, slot],
                       partner)
@@ -233,71 +238,52 @@
     def kept(j):
         return pltpu.make_async_copy(total.at[j, me % 4], place(j, side), keep.at[j])
 
-    def planes_of(c):
-        return pl.ds(c * planes, planes)
-
-    def edge_copies(c):
-        return (
-            remote(edge_z.at[c, 0], halo_z.at[c, 0], ez_s.at[c, 0], ez_r.at[c, 0], z_next),
-            remote(edge_z.at[c, 1], halo_z.at[c, 1], ez_s.at[c, 1], ez_r.at[c, 1], z_prev),
-            remote(field.at[planes_of(c), rows_y - 8 :, :], halo_y.at[c, 0], ey_s.at[c, 0],
-                   ey_r.at[c, 0], y_next, "gy"),
-            remote(field.at[planes_of(c), 0:8, :], halo_y.at[c, 1], ey_s.at[c, 1],
-                   ey_r.at[c, 1], y_prev, "gy"),
-        )
-
-    def corner_copies(c):
-        return (
-            remote(halo_z.at[c], corner.at[c, 0], ec_s.at[c, 0], ec_r.at[c, 0], y_next, "gy"),
-            remote(halo_z.at[c], corner.at[c, 1], ec_s.at[c, 1], ec_r.at[c, 1], y_prev, "gy"),
-        )
-
-    def out_copy(c):
-        return pltpu.make_async_copy(field.at[planes_of(c)], out.at[c], out_s.at[c])
-
-    def send_edges(c):
-        @pl.loop(0, planes)
-        def _(x):
-            at = pl.ds(pl.multiple_of(x * 8, 8), 8)
-            tail = field[c * planes + x, :, width - 128 :]
-            edge_z[c, 0, at, :] = jnp.transpose(tail)[120:128]
-            edge_z[c, 1, at, :] = jnp.transpose(field[c * planes + x, :, 0:128])[0:8]
-        for copy in edge_copies(c):
+    def edge_copies(p):
+        copies = [
+            remote(edge_z.at[p, 0], halo_z.at[p, 0], ez_s.at[p, 0], ez_r.at[p, 0], z_next),
+            remote(edge_z.at[p, 1], halo_z.at[p, 1], ez_s.at[p, 1], ez_r.at[p, 1], z_prev),
+            remote(field.at[p, rows_y - 8 :, :], halo_y.at[p, 0], ey_s.at[p, 0],
+                   ey_r.at[p, 0], {"gy": y_next}),
+            remote(field.at[p, 0:8, :], halo_y.at[p, 1], ey_s.at[p, 1],
+                   ey_r.at[p, 1], {"gy": y_prev}),
+        ]
+        for n, peer in enumerate(diagonals):
+            zed, why = n // 2, n % 2
+            copies.append(remote(edge_z.at[p, zed], corner.at[p, why, zed], ec_s.at[p, n],
+                                 ec_r.at[p, n], peer))
+        return copies
+
+    def out_copy(p):
+        return pltpu.make_async_copy(field.at[p], out.at[p // planes, p % planes], out_s.at[p])
+
+    def send_edges(p):
+        edge_z[p, 0] = jnp.transpose(field[p, :, width - 128 :])[120:128]
+        edge_z[p, 1] = jnp.transpose(field[p, :, 0:128])[0:8]
+        for copy in edge_copies(p):
             copy.start()
-        out_copy(c).start()
-
-    def send_corners(c):
-        first, second, _, _ = edge_copies(c)
-        first.wait_recv()
-        second.wait_recv()
-        for copy in corner_copies(c):
-            copy.start()
-
-    def prepare(c):
-        _, _, third, fourth = edge_copies(c)
-        third.wait_recv()
-        fourth.wait_recv()
-        for copy in corner_copies(c):
+        out_copy(p).start()
+
+    def prepare(p):
+        for copy in edge_copies(p):
             copy.wait_recv()
         none = jnp.zeros((112, 128), F32)
 
-        @pl.loop(0, planes)
-        def _(x):
-            at = pl.ds(pl.multiple_of(x * 8, 8), 8)
-            main = pl.ds(pl.multiple_of(x * rows_y, rows_y), rows_y)
-            edge = pl.ds(pl.multiple_of(planes * rows_y + x * 16, 16), 16)
-
-            def unfold(low, high):
-                return jnp.transpose(jnp.concatenate([low, high, none], axis=0))
-
-            fhi[main, 0:width], flo[main, 0:width] = split(field[c * planes + x])
-            fhi[main, width:], flo[main, width:] = split(
-                unfold(halo_z[c, 0, at, :], halo_z[c, 1, at, :]))
-            fhi[edge, 0:width], flo[edge, 0:width] = split(
-                jnp.concatenate([halo_y[c, 0, x], halo_y[c, 1, x]], axis=0))
-            low = unfold(corner[c, 0, 0, at, :], corner[c, 0, 1, at, :])[rows_y - 8 :]
-            high = unfold(corner[c, 1, 0, at, :], corner[c, 1, 1, at, :])[0:8]
-            fhi[edge, width:], flo[edge, width:] = split(jnp.concatenate([low, high], axis=0))
+        def unfold(low, high):
+            return jnp.transpose(jnp.concatenate([low, high, none], axis=0))
+
+        def put(rows, lanes, value):
+            high, low = split(value)
+            fboth[rows, lanes] = high
+            fboth[rows.start + body : rows.stop + body, lanes] = low
+
+        main, edge = slice(0, rows_y), slice(rows_y, body)
+        inner, outer = slice(0, width), slice(width, width + 128)
+        put(main, inner, field[p])
+        put(main, outer, unfold(halo_z[p, 0], halo_z[p, 1]))
+        put(edge, inner, jnp.concatenate([halo_y[p, 0], halo_y[p, 1]], axis=0))
+        low = unfold(corner[p, 0, 0], corner[p, 0, 1])[rows_y - 8 :]
+        high = unfold(corner[p, 1, 0], corner[p, 1, 1])[0:8]
+        put(edge, outer, jnp.concatenate([low, high], axis=0))
 
     def lanes_of(u):
         return pl.ds(pl.multiple_of(u * chunk, chunk), chunk)
@@ -309,6 +295,8 @@
 
     def weigh(u):
         at = lanes_of(u)
+        for x, weight in enumerate(spline_weights(offs[0:1, at])):
+            wxs[x, :, at] = weight
         wy = spline_weights(offs[1:2, at])
         wz = spline_weights(offs[2:3, at])
         first_y = first_cell(0, gy * rows_y, gy_count * rows_y, at)
@@ -333,56 +321,86 @@
             rows = pl.ds(pl.multiple_of(tile * 16, 16), 16)
             py[rows, at] = dense(spot - first_y, wy)
 
-    def interpolate(c, u):
+    def interpolate(p, u):
+        c, x = p // planes, p % planes
         at = lanes_of(u)
-        wx = spline_weights(offs[0:1, at])
-        high = fhi[...]
-        field_z = (dot(high, pzhi[:, at]) + dot(flo[...], pzhi[:, at]) + dot(high, pzlo[:, at]))
-        value = jnp.zeros((1, chunk), F32)
-        for x in range(planes):
-            begin = planes * rows_y + x * 16
-            part = jnp.sum(field_z[x * rows_y : (x + 1) * rows_y] * py[8 : 8 + rows_y, at],
-                           axis=0, keepdims=True)
-            ends = (field_z[begin : begin + 8] * py[0:8, at]
-                    + field_z[begin + 8 : begin + 16] * py[8 + rows_y :, at])
-            value = value + (part + jnp.sum(ends, axis=0, keepdims=True)) * wx[x]
+        both = dot(fboth[...], pzhi[:, at])
+        field_z = both[0:body] + both[body:] + dot(fboth[0:body], pzlo[:, at])
+        value = jnp.sum(field_z[0:rows_y] * py[8 : 8 + rows_y, at], axis=0, keepdims=True)
+        ends = (field_z[rows_y : rows_y + 8] * py[0:8, at]
+                + field_z[rows_y + 8 :] * py[8 + rows_y :, at])
+        value = (value + jnp.sum(ends, axis=0, keepdims=True)) * wxs[x, :, at]
         slot = lax.broadcasted_iota(jnp.int32, (1, chunk), 1) + u * chunk
-        vals[c, :, at] = jnp.where(slot < count_ref[0], value, 0.0)
+        vals[c, :, at] = vals[c, :, at] + jnp.where(slot < count_ref[0], value, 0.0)
 
     def finish():
-        @pl.loop(0, components)
-        def _(c):
-            for copy in edge_copies(c) + corner_copies(c):
+        @pl.loop(0, pieces)
+        def _(p):
+            for copy in edge_copies(p):
                 copy.wait_send()
-            out_copy(c).wait()
+            out_copy(p).wait()
+
+    vals[...] = jnp.zeros(vals.shape, F32)
 
     @pl.when(jnp.logical_not(is_hub))
     def _():
-        @pl.loop(0, chunks)
+        pl.semaphore_wait(barrier, 11)
+
+        @pl.loop(0, DIRECT)
         def _(j):
             give(j, side, 0, hub_same).start()
             give(j, 1 - side, 1, hub_other).start()
 
+        @pl.loop(DIRECT, chunks)
+        def _(j):
+            give(j, 1 - side, 1, leaf_other).start()
+
+        give(DIRECT, side, 0, hub_same).start()
+        give(DIRECT + 1, side, 0, hub_same).start()
+
         pl.loop(0, groups)(weigh)
 
-        @pl.loop(0, components)
-        def _(c):
-            @pl.loop(0, per_part)
+        def pass_on(j):
+            arrival(j, leaf_other % 4).wait_recv()
+            relay(j).start()
+
+            @pl.when(j + 2 < chunks)
+            def _():
+                give(j + 2, side, 0, hub_same).start()
+
+        pl.loop(DIRECT, FIRST_RELAYS)(pass_on)
+
+        @pl.loop(0, pieces)
+        def _(p):
+            @pl.when(p > 0)
+            def _():
+                @pl.loop(0, RELAYS)
+                def _(n):
+                    j = FIRST_RELAYS + (p - 1) * RELAYS + n
+
+                    @pl.when(j < chunks)
+                    def _():
+                        pass_on(j)
+
+            @pl.loop(0, SUB)
             def _(n):
-                taken(c * per_part + n, side).wait_recv()
-                taken(c * per_part + n, 1 - side).wait_recv()
-            send_edges(c)
-            send_corners(c)
-            prepare(c)
+                taken(p * SUB + n, side).wait_recv()
+                taken(p * SUB + n, 1 - side).wait_recv()
+            send_edges(p)
+            prepare(p)
 
             @pl.loop(0, groups)
             def _(u):
-                interpolate(c, u)
+                interpolate(p, u)
 
         @pl.loop(0, chunks)
         def _(j):
             give(j, side, 0, hub_same).wait_send()
             give(j, 1 - side, 1, hub_other).wait_send()
+
+            @pl.when(j >= DIRECT)
+            def _():
+                relay(j).wait_send()
         finish()
 
     def first_stage(j):
@@ -425,63 +443,98 @@
 
         zsend[j] = product(1 - half)
         cross(j).start()
-        zown[j % 2] = product(half)
+        zown[j % (LAG + 1)] = product(half)
 
     def second_stage(j):
         cross(j).wait_recv()
+        mine = j % (LAG + 1)
+        targets = []
         for target in range(4):
             lanes = slice(target * each, target * each + each)
-            pieces = []
+            terms = []
             for m in range(parts):
                 rows = slice(m * lines, m * lines + lines)
-                pieces.append(zown[j % 2, rows, lanes] + zrecv[j, rows, lanes])
-            hi, lo = split(jnp.concatenate(pieces, axis=1))
-            total[j, target] = dot(hi, perm[...]) + dot(lo, perm[...])
+                terms.append(zown[mine, rows, lanes] + zrecv[j, rows, lanes])
+            targets.append(jnp.concatenate(terms, axis=1))
+        hi, lo = split(jnp.concatenate(targets, axis=0))
+        both = dot(jnp.concatenate([hi, lo], axis=0), perm[...])
+        for target in range(4):
+            at, low = target * lines, (4 + target) * lines
+            total[j, target] = both[at : at + lines] + both[low : low + lines]
         hand(j, 0, leaf_same).start()
         hand(j, 1, leaf_other).start()
         hand(j, 2, hub_other).start()
         kept(j).start()
+
+    def finish_piece(p):
+        @pl.loop(0, SUB)
+        def _(n):
+            kept(p * SUB + n).wait()
+            taken(p * SUB + n, 1 - side).wait_recv()
+        send_edges(p)
+
+    def spread(step):
+        p, turn = step // SUB, step % SUB
+
+        @pl.when(turn == 0)
+        def _():
+            prepare(p)
+
+        @pl.loop(0, share)
+        def _(n):
+            interpolate(p, turn * share + n)
 
     @pl.when(is_hub)
     def _():
         @pl.loop(0, chunks)
         def _(j):
             own(j).start()
+        pl.semaphore_wait(barrier, 12)
+
+        @pl.loop(0, AHEAD)
+        def _(j):
             give(j, 1 - side, 0, hub_other).start()
 
-        @pl.loop(0, chunks + 1)
+        pl.loop(0, groups)(weigh)
+        first_edge = SUB - 1 + LAG + 2
+        first_step = first_edge + 2
+        steps = chunks + LAG
+
+        @pl.loop(0, steps)
         def _(t):
             @pl.when(t < chunks)
             def _():
                 first_stage(t)
 
-            @pl.when(t > 0)
+            @pl.when(t + AHEAD < chunks)
             def _():
-                second_stage(t - 1)
-
-            @pl.when(t < groups)
+                give(t + AHEAD, 1 - side, 0, hub_other).start()
+
+            @pl.when(t >= LAG)
             def _():
-                weigh(t)
-
-        @pl.loop(0, components)
-        def _(c):
-            @pl.loop(0, per_part)
-            def _(n):
-                kept(c * per_part + n).wait()
-                taken(c * per_part + n, 1 - side).wait_recv()
-            send_edges(c)
-
-        @pl.loop(0, components)
-        def _(c):
-            send_corners(c)
-
-        @pl.loop(0, components)
-        def _(c):
-            prepare(c)
-
-            @pl.loop(0, groups)
-            def _(u):
-                interpolate(c, u)
+                second_stage(t - LAG)
+
+            @pl.when((t >= first_edge) & ((t - first_edge) % SUB == 0))
+            def _():
+                finish_piece((t - first_edge) // SUB)
+
+            @pl.when(t >= first_step)
+            def _():
+                spread(t - first_step)
+
+        done = (steps - 1 - first_edge) // SUB + 1
+
+        @pl.loop(steps - first_step, done * SUB)
+        def _(step):
+            spread(step)
+
+        @pl.loop(done, pieces)
+        def _(p):
+            finish_piece(p)
+
+        @pl.loop(done * SUB, pieces * SUB)
+        def _(step):
+            spread(step)
 
         @pl.loop(0, chunks)
         def _(j):
@@ -497,7 +550,8 @@
     components, _, planes, rows_y, width = spectrum.shape
     slots = cells.shape[1]
     lines = rows_y // (2 * SUB)
-    chunks = components * planes * SUB
+    pieces = components * planes
+    chunks = pieces * SUB
     factor, tcos, tsin, whi, wlo, perm = tables
     sign = np.ones((2, 8, 1), np.float32)
     sign[1, 1::2] = -1.0
@@ -505,7 +559,6 @@
     tcos, tsin = tcos[None] * sign, tsin[None] * sign
     dma = pltpu.SemaphoreType.DMA
     vmem = pl.BlockSpec(memory_space=pltpu.VMEM)
-    body = planes * (rows_y + 16)
     out, values = pl.pallas_call(
         hub_kernel,
         out_shape=(jax.ShapeDtypeStruct((components, planes, rows_y, width), F32),
@@ -517,21 +570,21 @@
             pltpu.VMEM((chunks, 4, 2, lines, width), F32),
             pltpu.VMEM((8 * lines, 2 * width), BF16),
             pltpu.VMEM((8 * lines, 2 * width), BF16),
-            pltpu.VMEM((2, 8 * lines, width // 2), F32),
+            pltpu.VMEM((LAG + 1, 8 * lines, width // 2), F32),
             pltpu.VMEM((chunks, 8 * lines, width // 2), F32),
             pltpu.VMEM((chunks, 8 * lines, width // 2), F32),
             pltpu.VMEM((chunks, 4, lines, width), F32),
-            pltpu.VMEM((components * planes, rows_y, width), F32),
-            pltpu.VMEM((components, 2, planes * 8, 128), F32),
-            pltpu.VMEM((components, 2, planes * 8, 128), F32),
-            pltpu.VMEM((components, 2, planes, 8, width), F32),
-            pltpu.VMEM((components, 2, 2, planes * 8, 128), F32),
-            pltpu.VMEM((body, width + 128), BF16),
-            pltpu.VMEM((body, width + 128), BF16),
+            pltpu.VMEM((pieces, rows_y, width), F32),
+            pltpu.VMEM((pieces, 2, 8, 128), F32),
+            pltpu.VMEM((pieces, 2, 8, 128), F32),
+            pltpu.VMEM((pieces, 2, 8, width), F32),
+            pltpu.VMEM((pieces, 2, 2, 8, 128), F32),
+            pltpu.VMEM((2 * (rows_y + 16), width + 128), BF16),
             pltpu.VMEM((width + 128, slots), BF16),
             pltpu.VMEM((width + 128, slots), BF16),
             pltpu.VMEM((rows_y + 16, slots), F32),
-            dma((chunks, 2)),
+            pltpu.VMEM((planes, 1, slots), F32),
+            dma((chunks, 3)),
             dma((chunks, 4)),
             dma((chunks,)),
             dma((chunks,)),
@@ -539,7 +592,7 @@
             dma((chunks, 2)),
             dma((chunks,)),
             dma((chunks,)),
-        ] + [dma((components, 2))] * 6 + [dma((components,))],
+        ] + [dma((pieces, 2))] * 4 + [dma((pieces, 4))] * 2 + [dma((pieces,))],
         compiler_params=pltpu.CompilerParams(
             collective_id=0, has_side_effects=True, vmem_limit_bytes=63 << 20),
     )(spectrum, counts, cells, offsets, factor, tcos, tsin, whi, wlo, perm)
@@ -701,8 +754,8 @@
     tables = line_tables(parts, rows_z) if tiled else None
     exchange = functools.partial(
         lax.all_to_all, axis_name="gz", split_axis=0, concat_axis=0, tiled=True)
-    if (parts == 8 and tiled and rows_y == 128 and cells.shape[1] % 256 == 0
-            and cells.shape[1] // 256 <= components * planes * SUB):
+    if (parts == 8 and tiled and rows_y == 128 and planes == 4 and lax.axis_size("gy") > 2
+            and cells.shape[1] % (256 * SUB) == 0):
         return hub_program(spectrum, cells, offsets, counts, tables)
     blocks = []
     for c in range(components):

time: 217 us -> 269 us (1.24); the launches traced: 216 us -> 265 us
  Pallas kernels: 210 us -> 258 us
    pallas_call x1, Pallas kernels: 210 us -> 258 us  [hub_program(): pl.pallas_call(hub_kernel, out_shape=(jax.ShapeDtypeStruct((components, p...]
where the time goes in v1:
time: 269 us; the launch traced here: 265 us
  Pallas kernels  258 us (96%)
  local copies, waits for them, and re-layouts  5.22 us (2%)
    pallas_call x1, Pallas kernels, hub_program(): pl.pallas_call(hub_kernel, out_shape=(jax.ShapeDtypeStruct((components, p...  258 us

profile of v1, /device:TPU:8, one launch (start us, length us, event | category | flops | bytes accessed | tf_op | source)
XLA Modules:
  0.0 265.0 jit_solution(4087990057908076760)
XLA Ops:
  1.3 258.5 %shard_map.113 = (f32[3,4,128,512]{3,2,1,0:T(8,128)}, f32[3,1,2048]{2,1,0:T(1,128)}) custom-call(f32[3,2,4,128,512]{4,3,2,1,0:T(8,128)} %spec.1, s32[1]{0:T(128)S(6)} %copy.16.count_ref, s32[2,2048]{1,0:T(2,128)} %cells.1, f32[3,2048]{1,0:T(4,128)} %offs.1, f32[2,4,512]{2,1,0:T(4,128)} %constant.12.clone.factor, f32[2,8,512]{2,1,0:T(8,128)} %constant.13.clone.tcos, ...), custom_call_target="tpu_custom_call" | custom-call | tf_op jit(solution)/shard_map/pallas_call | solution.py:562
  259.7 1.4 copy.14
  261.1 3.9 %copy.17 = f32[3,4,128,512]{3,2,1,0:T(8,128)} copy(f32[3,4,128,512]{3,2,1,0:T(8,128)} %get-tuple-element.8) | data formatting | bytes 6291456

commit v2 on v1

--- a/solution.py
+++ b/solution.py
@@ -136,11 +136,11 @@
 
 
 SUB = 4
-DIRECT = 6
-AHEAD = 6
+DIRECT = 2
+AHEAD = 2
+EARLY = 6
 LAG = 2
-FIRST_RELAYS = 16
-RELAYS = 6
+DEPTH = 2
 
 
 def hub_kernel(spec, count_ref, cells, offs, factor, tcos, tsin, whi, wlo, perm, out, vals,
@@ -340,67 +340,99 @@
                 copy.wait_send()
             out_copy(p).wait()
 
+    def spread(step):
+        p, turn = step // SUB, step % SUB
+
+        @pl.when(turn == 0)
+        def _():
+            prepare(p)
+
+        @pl.loop(0, share)
+        def _(n):
+            interpolate(p, turn * share + n)
+
     vals[...] = jnp.zeros(vals.shape, F32)
+
+    @pl.when(is_hub)
+    def _():
+        @pl.loop(0, chunks)
+        def _(j):
+            own(j).start()
+
+    pl.loop(0, groups)(weigh)
 
     @pl.when(jnp.logical_not(is_hub))
     def _():
         pl.semaphore_wait(barrier, 11)
 
-        @pl.loop(0, DIRECT)
-        def _(j):
-            give(j, side, 0, hub_same).start()
-            give(j, 1 - side, 1, hub_other).start()
-
-        @pl.loop(DIRECT, chunks)
+        @pl.loop(DIRECT, EARLY)
         def _(j):
             give(j, 1 - side, 1, leaf_other).start()
 
-        give(DIRECT, side, 0, hub_same).start()
-        give(DIRECT + 1, side, 0, hub_same).start()
-
-        pl.loop(0, groups)(weigh)
+        first_edge = SUB - 1 + LAG + DEPTH + 4
+        first_step = first_edge + 3
+
+        def same(j):
+            return give(j, side, 0, hub_same)
+
+        def sent(j):
+            same(j).wait_send()
+            give(j, 1 - side, 1, hub_other).wait_send()
+
+            @pl.when(j >= DIRECT)
+            def _():
+                relay(j).wait_send()
 
         def pass_on(j):
-            arrival(j, leaf_other % 4).wait_recv()
-            relay(j).start()
-
-            @pl.when(j + 2 < chunks)
-            def _():
-                give(j + 2, side, 0, hub_same).start()
-
-        pl.loop(DIRECT, FIRST_RELAYS)(pass_on)
-
-        @pl.loop(0, pieces)
-        def _(p):
-            @pl.when(p > 0)
-            def _():
-                @pl.loop(0, RELAYS)
-                def _(n):
-                    j = FIRST_RELAYS + (p - 1) * RELAYS + n
-
-                    @pl.when(j < chunks)
-                    def _():
-                        pass_on(j)
-
+            @pl.when(j >= DEPTH)
+            def _():
+                sent(j - DEPTH)
+
+            same(j).start()
+
+            @pl.when(j + EARLY < chunks)
+            def _():
+                give(j + EARLY, 1 - side, 1, leaf_other).start()
+
+            @pl.when(j < DIRECT)
+            def _():
+                give(j, 1 - side, 1, hub_other).start()
+
+            @pl.when(j >= DIRECT)
+            def _():
+                arrival(j, leaf_other % 4).wait_recv()
+                relay(j).start()
+
+        def finish_piece(p):
             @pl.loop(0, SUB)
             def _(n):
                 taken(p * SUB + n, side).wait_recv()
                 taken(p * SUB + n, 1 - side).wait_recv()
             send_edges(p)
-            prepare(p)
-
-            @pl.loop(0, groups)
-            def _(u):
-                interpolate(p, u)
-
-        @pl.loop(0, chunks)
+
+        steps = (pieces - 1) * SUB + first_edge + 1
+
+        @pl.loop(0, steps)
+        def _(t):
+            @pl.when(t < chunks)
+            def _():
+                pass_on(t)
+
+            @pl.when((t >= first_edge) & ((t - first_edge) % SUB == 0))
+            def _():
+                finish_piece((t - first_edge) // SUB)
+
+            @pl.when(t >= first_step)
+            def _():
+                spread(t - first_step)
+
+        @pl.loop(steps - first_step, chunks)
+        def _(step):
+            spread(step)
+
+        @pl.loop(chunks - DEPTH, chunks)
         def _(j):
-            give(j, side, 0, hub_same).wait_send()
-            give(j, 1 - side, 1, hub_other).wait_send()
-
-            @pl.when(j >= DIRECT)
-            def _():
-                relay(j).wait_send()
+            sent(j)
         finish()
 
     def first_stage(j):
@@ -473,31 +505,16 @@
             taken(p * SUB + n, 1 - side).wait_recv()
         send_edges(p)
 
-    def spread(step):
-        p, turn = step // SUB, step % SUB
-
-        @pl.when(turn == 0)
-        def _():
-            prepare(p)
-
-        @pl.loop(0, share)
-        def _(n):
-            interpolate(p, turn * share + n)
-
     @pl.when(is_hub)
     def _():
-        @pl.loop(0, chunks)
-        def _(j):
-            own(j).start()
         pl.semaphore_wait(barrier, 12)
 
         @pl.loop(0, AHEAD)
         def _(j):
             give(j, 1 - side, 0, hub_other).start()
 
-        pl.loop(0, groups)(weigh)
         first_edge = SUB - 1 + LAG + 2
-        first_step = first_edge + 2
+        first_step = first_edge + 5
         steps = chunks + LAG
 
         @pl.loop(0, steps)
@@ -524,7 +541,7 @@
 
         done = (steps - 1 - first_edge) // SUB + 1
 
-        @pl.loop(steps - first_step, done * SUB)
+        @pl.loop(steps - first_step, (done - 1) * SUB)
         def _(step):
             spread(step)
 
@@ -532,7 +549,7 @@
         def _(p):
             finish_piece(p)
 
-        @pl.loop(done * SUB, pieces * SUB)
+        @pl.loop((done - 1) * SUB, chunks)
         def _(step):
             spread(step)
 

time: 269 us -> 181 us (0.67)
  Pallas kernels: 258 us -> 173 us
    pallas_call x1, Pallas kernels: 258 us -> 173 us  [hub_program(): pl.pallas_call(hub_kernel, out_shape=(jax.ShapeDtypeStruct((components, p...]
where the time goes in v2:
time: 181 us; the launch traced here: 179 us
  Pallas kernels  173 us (96%)
  local copies, waits for them, and re-layouts  5.22 us (3%)
    pallas_call x1, Pallas kernels, hub_program(): pl.pallas_call(hub_kernel, out_shape=(jax.ShapeDtypeStruct((components, p...  173 us
    unnamed x2, local copies, waits for them, and re-layouts  5.22 us

profile of v2, /device:TPU:8, one launch (start us, length us, event | category | flops | bytes accessed | tf_op | source)
XLA Modules:
  0.0 179.1 jit_solution(17898522414542263932)
XLA Ops:
  1.3 172.6 %shard_map.113 = (f32[3,4,128,512]{3,2,1,0:T(8,128)}, f32[3,1,2048]{2,1,0:T(1,128)}) custom-call(f32[3,2,4,128,512]{4,3,2,1,0:T(8,128)} %spec.1, s32[1]{0:T(128)S(6)} %copy.16.count_ref, s32[2,2048]{1,0:T(2,128)} %cells.1, f32[3,2048]{1,0:T(4,128)} %offs.1, f32[2,4,512]{2,1,0:T(4,128)} %constant.12.clone.factor, f32[2,8,512]{2,1,0:T(8,128)} %constant.13.clone.tcos, ...), custom_call_target="tpu_custom_call" | custom-call | tf_op jit(solution)/shard_map/pallas_call | solution.py:579
  173.9 1.4 copy.14
  175.3 3.9 %copy.17 = f32[3,4,128,512]{3,2,1,0:T(8,128)} copy(f32[3,4,128,512]{3,2,1,0:T(8,128)} %get-tuple-element.8) | data formatting | bytes 6291456

commit v3 on v2

--- a/solution.py
+++ b/solution.py
@@ -144,10 +144,10 @@
 
 
 def hub_kernel(spec, count_ref, cells, offs, factor, tcos, tsin, whi, wlo, perm, out, vals,
-               xbuf, yhi, ylo, zown, zsend, zrecv, total, field, edge_z, halo_z, halo_y, corner,
-               fboth, pzhi, pzlo, py, wxs,
-               send_a, recv_a, cross_s, cross_r, dist_s, dist_r, loc, keep,
-               ez_s, ez_r, ey_s, ey_r, ec_s, ec_r, out_s):
+               xbuf, yhi, ylo, zown, zsend, zrecv, rim_out, rim_in, total, field, halo_y,
+               fboth, pzhi, pzlo, py, wxs, acc,
+               send_a, recv_a, cross_s, cross_r, rim_s, rim_r, dist_s, dist_r, loc, keep,
+               halo_s, halo_r, out_s):
     components, _, planes, rows_y, width = spec.shape
     lines = rows_y // (2 * SUB)
     pieces = components * planes
@@ -169,23 +169,24 @@
     leaf_same = 6 * half + side
     leaf_other = 6 * half + (1 - side)
     partner = 4 - 2 * half + side
-    z_next, z_prev = lax.rem(me + 1, 8), lax.rem(me + 7, 8)
     gy, gy_count = lax.axis_index("gy"), lax.axis_size("gy")
     y_next, y_prev = lax.rem(gy + 1, gy_count), lax.rem(gy + gy_count - 1, gy_count)
-    diagonals = [{"gz": z, "gy": y} for z in (z_next, z_prev) for y in (y_next, y_prev)]
 
     barrier = pltpu.get_barrier_semaphore()
 
     def greet(peer):
         pl.semaphore_signal(barrier, inc=1, device_id=peer, device_id_type=MESH)
 
-    for peer in [{"gz": z_next}, {"gz": z_prev}, {"gy": y_next}, {"gy": y_prev}] + diagonals:
-        greet(peer)
+    greet({"gz": 2 + 2 * half, "gy": y_next})
+    greet({"gz": 3 + 2 * half, "gy": y_prev})
 
     @pl.when(is_hub)
     def _():
         for peer in (leaf_same, leaf_other, hub_other, partner):
             greet({"gz": peer})
+        beside = jnp.where(side == 1, y_next, y_prev)
+        for target in range(4):
+            greet({"gz": 4 * half + target, "gy": beside})
 
     @pl.when(jnp.logical_not(is_hub))
     def _():
@@ -224,6 +225,9 @@
     def cross(j):
         return remote(zsend.at[j], zrecv.at[j], cross_s.at[j], cross_r.at[j], partner)
 
+    def rim(j):
+        return remote(rim_out.at[j], rim_in.at[j], rim_s.at[j], rim_r.at[j], partner)
+
     def place(j, which):
         return field.at[j // SUB, rows_of(j, which), :]
 
@@ -238,52 +242,41 @@
     def kept(j):
         return pltpu.make_async_copy(total.at[j, me % 4], place(j, side), keep.at[j])
 
-    def edge_copies(p):
-        copies = [
-            remote(edge_z.at[p, 0], halo_z.at[p, 0], ez_s.at[p, 0], ez_r.at[p, 0], z_next),
-            remote(edge_z.at[p, 1], halo_z.at[p, 1], ez_s.at[p, 1], ez_r.at[p, 1], z_prev),
-            remote(field.at[p, rows_y - 8 :, :], halo_y.at[p, 0], ey_s.at[p, 0],
-                   ey_r.at[p, 0], {"gy": y_next}),
-            remote(field.at[p, 0:8, :], halo_y.at[p, 1], ey_s.at[p, 1],
-                   ey_r.at[p, 1], {"gy": y_prev}),
-        ]
-        for n, peer in enumerate(diagonals):
-            zed, why = n // 2, n % 2
-            copies.append(remote(edge_z.at[p, zed], corner.at[p, why, zed], ec_s.at[p, n],
-                                 ec_r.at[p, n], peer))
-        return copies
+    def border(p, target, last):
+        if last:
+            rows, peer = total.at[p * SUB + SUB - 1, target, lines - 8 :, :], y_next
+        else:
+            rows, peer = total.at[p * SUB, target, 0:8, :], y_prev
+        at = 0 if last else 1
+        return remote(rows, halo_y.at[p, at], halo_s.at[p, target], halo_r.at[p, at],
+                      {"gz": 4 * half + target, "gy": peer})
 
     def out_copy(p):
-        return pltpu.make_async_copy(field.at[p], out.at[p // planes, p % planes], out_s.at[p])
-
-    def send_edges(p):
-        edge_z[p, 0] = jnp.transpose(field[p, :, width - 128 :])[120:128]
-        edge_z[p, 1] = jnp.transpose(field[p, :, 0:128])[0:8]
-        for copy in edge_copies(p):
-            copy.start()
+        return pltpu.make_async_copy(field.at[p, :, 0:width], out.at[p // planes, p % planes],
+                                     out_s.at[p])
+
+    def prepare(p):
+        @pl.when(is_hub)
+        def _():
+            @pl.loop(0, SUB)
+            def _(n):
+                kept(p * SUB + n).wait()
+
+        @pl.when(jnp.logical_not(is_hub))
+        def _():
+            @pl.loop(0, SUB)
+            def _(n):
+                taken(p * SUB + n, side).wait_recv()
+
+        @pl.loop(0, SUB)
+        def _(n):
+            taken(p * SUB + n, 1 - side).wait_recv()
         out_copy(p).start()
-
-    def prepare(p):
-        for copy in edge_copies(p):
-            copy.wait_recv()
-        none = jnp.zeros((112, 128), F32)
-
-        def unfold(low, high):
-            return jnp.transpose(jnp.concatenate([low, high, none], axis=0))
-
-        def put(rows, lanes, value):
-            high, low = split(value)
-            fboth[rows, lanes] = high
-            fboth[rows.start + body : rows.stop + body, lanes] = low
-
-        main, edge = slice(0, rows_y), slice(rows_y, body)
-        inner, outer = slice(0, width), slice(width, width + 128)
-        put(main, inner, field[p])
-        put(main, outer, unfold(halo_z[p, 0], halo_z[p, 1]))
-        put(edge, inner, jnp.concatenate([halo_y[p, 0], halo_y[p, 1]], axis=0))
-        low = unfold(corner[p, 0, 0], corner[p, 0, 1])[rows_y - 8 :]
-        high = unfold(corner[p, 1, 0], corner[p, 1, 1])[0:8]
-        put(edge, outer, jnp.concatenate([low, high], axis=0))
+        border(p, 0, True).wait_recv()
+        border(p, 0, False).wait_recv()
+        fboth[0:rows_y], fboth[body : body + rows_y] = split(field[p])
+        fboth[rows_y:body], fboth[body + rows_y :] = split(
+            jnp.concatenate([halo_y[p, 0], halo_y[p, 1]], axis=0))
 
     def lanes_of(u):
         return pl.ds(pl.multiple_of(u * chunk, chunk), chunk)
@@ -330,14 +323,15 @@
         ends = (field_z[rows_y : rows_y + 8] * py[0:8, at]
                 + field_z[rows_y + 8 :] * py[8 + rows_y :, at])
         value = (value + jnp.sum(ends, axis=0, keepdims=True)) * wxs[x, :, at]
-        slot = lax.broadcasted_iota(jnp.int32, (1, chunk), 1) + u * chunk
-        vals[c, :, at] = vals[c, :, at] + jnp.where(slot < count_ref[0], value, 0.0)
+        acc[c, :, at] = acc[c, :, at] + value
 
     def finish():
+        slot = lax.broadcasted_iota(jnp.int32, (1, slots), 1)
+        for c in range(components):
+            vals[c : c + 1, :] = jnp.where(slot < count_ref[0], acc[c], 0.0)
+
         @pl.loop(0, pieces)
         def _(p):
-            for copy in edge_copies(p):
-                copy.wait_send()
             out_copy(p).wait()
 
     def spread(step):
@@ -351,7 +345,7 @@
         def _(n):
             interpolate(p, turn * share + n)
 
-    vals[...] = jnp.zeros(vals.shape, F32)
+    acc[...] = jnp.zeros(acc.shape, F32)
 
     @pl.when(is_hub)
     def _():
@@ -359,18 +353,15 @@
         def _(j):
             own(j).start()
 
-    pl.loop(0, groups)(weigh)
-
     @pl.when(jnp.logical_not(is_hub))
     def _():
-        pl.semaphore_wait(barrier, 11)
+        pl.semaphore_wait(barrier, 5)
 
         @pl.loop(DIRECT, EARLY)
         def _(j):
             give(j, 1 - side, 1, leaf_other).start()
 
-        first_edge = SUB - 1 + LAG + DEPTH + 4
-        first_step = first_edge + 3
+        first_step = SUB + LAG + DEPTH + 4
 
         def same(j):
             return give(j, side, 0, hub_same)
@@ -403,32 +394,19 @@
                 arrival(j, leaf_other % 4).wait_recv()
                 relay(j).start()
 
-        def finish_piece(p):
-            @pl.loop(0, SUB)
-            def _(n):
-                taken(p * SUB + n, side).wait_recv()
-                taken(p * SUB + n, 1 - side).wait_recv()
-            send_edges(p)
-
-        steps = (pieces - 1) * SUB + first_edge + 1
-
-        @pl.loop(0, steps)
+        @pl.loop(0, chunks + first_step)
         def _(t):
             @pl.when(t < chunks)
             def _():
                 pass_on(t)
 
-            @pl.when((t >= first_edge) & ((t - first_edge) % SUB == 0))
-            def _():
-                finish_piece((t - first_edge) // SUB)
+            @pl.when(t < groups)
+            def _():
+                weigh(t)
 
             @pl.when(t >= first_step)
             def _():
                 spread(t - first_step)
-
-        @pl.loop(steps - first_step, chunks)
-        def _(step):
-            spread(step)
 
         @pl.loop(chunks - DEPTH, chunks)
         def _(j):
@@ -475,10 +453,15 @@
 
         zsend[j] = product(1 - half)
         cross(j).start()
-        zown[j % (LAG + 1)] = product(half)
+        kept_part = product(half)
+        zown[j % (LAG + 1)] = kept_part
+        rim_out[j] = jnp.concatenate([jnp.transpose(kept_part[:, wide - 128 :])[127:128],
+                                      jnp.transpose(kept_part[:, 0:128])[0:1]], axis=0)
+        rim(j).start()
 
     def second_stage(j):
         cross(j).wait_recv()
+        rim(j).wait_recv()
         mine = j % (LAG + 1)
         targets = []
         for target in range(4):
@@ -488,33 +471,50 @@
                 rows = slice(m * lines, m * lines + lines)
                 terms.append(zown[mine, rows, lanes] + zrecv[j, rows, lanes])
             targets.append(jnp.concatenate(terms, axis=1))
+        count = parts * lines
+        lane = lax.broadcasted_iota(jnp.int32, (count, 128), 1)
+        theirs = jnp.transpose(jnp.concatenate([rim_in[j], jnp.zeros((126, count), F32)], axis=0))
+        ends = theirs + jnp.where(
+            lane == 0, pltpu.roll(zsend[j, :, wide - 128 :], 1, 1),
+            jnp.where(lane == 1, pltpu.roll(zsend[j, :, 0:128], 1, 1), 0.0))
+        targets.append(jnp.concatenate(
+            [ends[m * lines : m * lines + lines, 0:each] for m in range(parts)], axis=1))
         hi, lo = split(jnp.concatenate(targets, axis=0))
         both = dot(jnp.concatenate([hi, lo], axis=0), perm[...])
+        full = both[0 : 5 * lines] + both[5 * lines :]
+        ends = full[4 * lines :, 0:128]
+        lane = lax.broadcasted_iota(jnp.int32, (lines, 128), 1)
         for target in range(4):
-            at, low = target * lines, (4 + target) * lines
-            total[j, target] = both[at : at + lines] + both[low : low + lines]
+            at = target * lines
+            low = ends if target == 0 else pltpu.roll(full[at - lines : at, width - 128 :], 8, 1)
+            high = ends if target == 3 else pltpu.roll(full[at + lines : at + 2 * lines, 0:128], 8, 1)
+            total[j, target, :, 0:width] = full[at : at + lines]
+            total[j, target, :, width:] = jnp.where(
+                lane < 8, low, jnp.where(lane < 16, high, 0.0))
         hand(j, 0, leaf_same).start()
         hand(j, 1, leaf_other).start()
         hand(j, 2, hub_other).start()
         kept(j).start()
 
-    def finish_piece(p):
-        @pl.loop(0, SUB)
-        def _(n):
-            kept(p * SUB + n).wait()
-            taken(p * SUB + n, 1 - side).wait_recv()
-        send_edges(p)
+        @pl.when((side == 1) & (j % SUB == SUB - 1))
+        def _():
+            for target in range(4):
+                border(j // SUB, target, True).start()
+
+        @pl.when((side == 0) & (j % SUB == 0))
+        def _():
+            for target in range(4):
+                border(j // SUB, target, False).start()
 
     @pl.when(is_hub)
     def _():
-        pl.semaphore_wait(barrier, 12)
+        pl.semaphore_wait(barrier, 10)
 
         @pl.loop(0, AHEAD)
         def _(j):
             give(j, 1 - side, 0, hub_other).start()
 
-        first_edge = SUB - 1 + LAG + 2
-        first_step = first_edge + 5
+        first_step = SUB + LAG + 2
         steps = chunks + LAG
 
         @pl.loop(0, steps)
@@ -531,25 +531,15 @@
             def _():
                 second_stage(t - LAG)
 
-            @pl.when((t >= first_edge) & ((t - first_edge) % SUB == 0))
-            def _():
-                finish_piece((t - first_edge) // SUB)
+            @pl.when(t < groups)
+            def _():
+                weigh(t)
 
             @pl.when(t >= first_step)
             def _():
                 spread(t - first_step)
 
-        done = (steps - 1 - first_edge) // SUB + 1
-
-        @pl.loop(steps - first_step, (done - 1) * SUB)
-        def _(step):
-            spread(step)
-
-        @pl.loop(done, pieces)
-        def _(p):
-            finish_piece(p)
-
-        @pl.loop((done - 1) * SUB, chunks)
+        @pl.loop(steps - first_step, chunks)
         def _(step):
             spread(step)
 
@@ -557,9 +547,15 @@
         def _(j):
             give(j, 1 - side, 0, hub_other).wait_send()
             cross(j).wait_send()
+            rim(j).wait_send()
             hand(j, 0, leaf_same).wait_send()
             hand(j, 1, leaf_other).wait_send()
             hand(j, 2, hub_other).wait_send()
+
+        @pl.loop(0, pieces)
+        def _(p):
+            for target in range(4):
+                border(p, target, True).wait_send()
         finish()
 
 
@@ -579,7 +575,7 @@
     out, values = pl.pallas_call(
         hub_kernel,
         out_shape=(jax.ShapeDtypeStruct((components, planes, rows_y, width), F32),
-                   jax.ShapeDtypeStruct((components, 1, slots), F32)),
+                   jax.ShapeDtypeStruct((components, slots), F32)),
         in_specs=[pl.BlockSpec(memory_space=pl.ANY), pl.BlockSpec(memory_space=pltpu.SMEM)]
         + [vmem] * 8,
         out_specs=(pl.BlockSpec(memory_space=pl.ANY), vmem),
@@ -590,30 +586,35 @@
             pltpu.VMEM((LAG + 1, 8 * lines, width // 2), F32),
             pltpu.VMEM((chunks, 8 * lines, width // 2), F32),
             pltpu.VMEM((chunks, 8 * lines, width // 2), F32),
-            pltpu.VMEM((chunks, 4, lines, width), F32),
-            pltpu.VMEM((pieces, rows_y, width), F32),
-            pltpu.VMEM((pieces, 2, 8, 128), F32),
-            pltpu.VMEM((pieces, 2, 8, 128), F32),
-            pltpu.VMEM((pieces, 2, 8, width), F32),
-            pltpu.VMEM((pieces, 2, 2, 8, 128), F32),
+            pltpu.VMEM((chunks, 2, 8 * lines), F32),
+            pltpu.VMEM((chunks, 2, 8 * lines), F32),
+            pltpu.VMEM((chunks, 4, lines, width + 128), F32),
+            pltpu.VMEM((pieces, rows_y, width + 128), F32),
+            pltpu.VMEM((pieces, 2, 8, width + 128), F32),
             pltpu.VMEM((2 * (rows_y + 16), width + 128), BF16),
             pltpu.VMEM((width + 128, slots), BF16),
             pltpu.VMEM((width + 128, slots), BF16),
             pltpu.VMEM((rows_y + 16, slots), F32),
             pltpu.VMEM((planes, 1, slots), F32),
+            pltpu.VMEM((components, 1, slots), F32),
             dma((chunks, 3)),
             dma((chunks, 4)),
+            dma((chunks,)),
+            dma((chunks,)),
             dma((chunks,)),
             dma((chunks,)),
             dma((chunks, 3)),
             dma((chunks, 2)),
             dma((chunks,)),
             dma((chunks,)),
-        ] + [dma((pieces, 2))] * 4 + [dma((pieces, 4))] * 2 + [dma((pieces,))],
+            dma((pieces, 4)),
+            dma((pieces, 2)),
+            dma((pieces,)),
+        ],
         compiler_params=pltpu.CompilerParams(
             collective_id=0, has_side_effects=True, vmem_limit_bytes=63 << 20),
     )(spectrum, counts, cells, offsets, factor, tcos, tsin, whi, wlo, perm)
-    return out, values.reshape(components, slots)
+    return out, values
 
 
 def general_transform(real, imag):
@@ -772,7 +773,7 @@
     exchange = functools.partial(
         lax.all_to_all, axis_name="gz", split_axis=0, concat_axis=0, tiled=True)
     if (parts == 8 and tiled and rows_y == 128 and planes == 4 and lax.axis_size("gy") > 2
-            and cells.shape[1] % (256 * SUB) == 0):
+            and cells.shape[1] % (256 * SUB) == 0 and cells.shape[1] // 256 <= 8):
         return hub_program(spectrum, cells, offsets, counts, tables)
     blocks = []
     for c in range(components):

time: 181 us -> 173 us (0.956)
  Pallas kernels: 173 us -> 165 us
    pallas_call x1, Pallas kernels: 173 us -> 165 us  [hub_program(): pl.pallas_call(hub_kernel, out_shape=(jax.ShapeDtypeStruct((components, p...]
    unnamed x2 -> x4, local copies, waits for them, and re-layouts: 5.22 us -> 4.48 us
where the time goes in v3:
time: 173 us; the launch traced here: 171 us
  Pallas kernels  165 us (95%)
  local copies, waits for them, and re-layouts  4.48 us (3%)
    pallas_call x1, Pallas kernels, hub_program(): pl.pallas_call(hub_kernel, out_shape=(jax.ShapeDtypeStruct((components, p...  165 us
    unnamed x4, local copies, waits for them, and re-layouts  4.48 us

profile of v3, /device:TPU:8, one launch (start us, length us, event | category | flops | bytes accessed | tf_op | source)
XLA Modules:
  0.0 170.5 jit_solution(7411890561064871454)
XLA Ops:
  1.3 164.8 %shard_map.113 = (f32[3,4,128,512]{3,2,1,0:T(8,128)}, f32[3,2048]{1,0:T(4,128)}) custom-call(f32[3,2,4,128,512]{4,3,2,1,0:T(8,128)} %spec.1, s32[1]{0:T(128)S(6)} %copy.14.count_ref, s32[2,2048]{1,0:T(2,128)} %cells.1, f32[3,2048]{1,0:T(4,128)} %offs.1, f32[2,4,512]{2,1,0:T(4,128)} %constant.12.clone.factor, f32[2,8,512]{2,1,0:T(8,128)} %constant.13.clone.tcos, ...), custom_call_target="tpu_custom_call" | custom-call | tf_op jit(solution)/shard_map/pallas_call | solution.py:575
  166.0 0.0 copy-start
  166.1 3.9 %copy.15 = f32[3,4,128,512]{3,2,1,0:T(8,128)} copy(f32[3,4,128,512]{3,2,1,0:T(8,128)} %get-tuple-element.4) | data formatting | bytes 6291456
  169.9 0.0 copy-done
  169.9 0.6 copy.16
Async XLA Ops:
  166.0 3.9 %copy-start = (f32[3,2048]{1,0:T(4,128)S(1)}, f32[3,2048]{1,0:T(4,128)}, u32[]{:S(2)}) copy-start(f32[3,2048]{1,0:T(4,128)} %get-tuple-element.5) | copy-start | bytes 73732

commit v4 on v3

--- a/solution.py
+++ b/solution.py
@@ -143,11 +143,17 @@
 DEPTH = 2
 
 
-def hub_kernel(spec, count_ref, cells, offs, factor, tcos, tsin, whi, wlo, perm, out, vals,
+def hub_kernel(spec, count_ref, cells, offs, *rest):
+    sources, (out, vals), tables, held = rest[:6], rest[6:8], rest[8:14], rest[14:]
+    hub_body(spec, count_ref, cells, offs, sources, tables, out, vals, *held)
+
+
+def hub_body(spec, count_ref, cells, offs, sources, tables, out, vals, table_s,
                xbuf, yhi, ylo, zown, zsend, zrecv, rim_out, rim_in, total, field, halo_y,
                fboth, pzhi, pzlo, py, wxs, acc,
                send_a, recv_a, cross_s, cross_r, rim_s, rim_r, dist_s, dist_r, loc, keep,
                halo_s, halo_r, out_s):
+    factor, tcos, tsin, whi, wlo, perm = tables
     components, _, planes, rows_y, width = spec.shape
     lines = rows_y // (2 * SUB)
     pieces = components * planes
@@ -346,12 +352,16 @@
             interpolate(p, turn * share + n)
 
     acc[...] = jnp.zeros(acc.shape, F32)
+    table_copies = [pltpu.make_async_copy(source, table, table_s.at[n])
+                    for n, (source, table) in enumerate(zip(sources, tables))]
 
     @pl.when(is_hub)
     def _():
         @pl.loop(0, chunks)
         def _(j):
             own(j).start()
+        for copy in table_copies:
+            copy.start()
 
     @pl.when(jnp.logical_not(is_hub))
     def _():
@@ -514,6 +524,8 @@
         def _(j):
             give(j, 1 - side, 0, hub_other).start()
 
+        for copy in table_copies:
+            copy.wait()
         first_step = SUB + LAG + 2
         steps = chunks + LAG
 
@@ -572,14 +584,21 @@
     tcos, tsin = tcos[None] * sign, tsin[None] * sign
     dma = pltpu.SemaphoreType.DMA
     vmem = pl.BlockSpec(memory_space=pltpu.VMEM)
+    hbm = pl.BlockSpec(memory_space=pltpu.HBM)
     out, values = pl.pallas_call(
         hub_kernel,
-        out_shape=(jax.ShapeDtypeStruct((components, planes, rows_y, width), F32),
-                   jax.ShapeDtypeStruct((components, slots), F32)),
-        in_specs=[pl.BlockSpec(memory_space=pl.ANY), pl.BlockSpec(memory_space=pltpu.SMEM)]
-        + [vmem] * 8,
-        out_specs=(pl.BlockSpec(memory_space=pl.ANY), vmem),
+        out_shape=(pltpu.VMEM((components, planes, rows_y, width), F32),
+                   pltpu.VMEM((components, slots), F32)),
+        in_specs=[hbm, pl.BlockSpec(memory_space=pltpu.SMEM), vmem, vmem] + [hbm] * 6,
+        out_specs=(vmem, vmem),
         scratch_shapes=[
+            pltpu.VMEM((2, 4, width), F32),
+            pltpu.VMEM((2, 8, width), F32),
+            pltpu.VMEM((2, 8, width), F32),
+            pltpu.VMEM((2 * width, width), BF16),
+            pltpu.VMEM((2 * width, width), BF16),
+            pltpu.VMEM((width, width), BF16),
+            dma((6,)),
             pltpu.VMEM((chunks, 4, 2, lines, width), F32),
             pltpu.VMEM((8 * lines, 2 * width), BF16),
             pltpu.VMEM((8 * lines, 2 * width), BF16),
@@ -612,7 +631,7 @@
             dma((pieces,)),
         ],
         compiler_params=pltpu.CompilerParams(
-            collective_id=0, has_side_effects=True, vmem_limit_bytes=63 << 20),
+            collective_id=0, has_side_effects=True, vmem_limit_bytes=56 << 20),
     )(spectrum, counts, cells, offsets, factor, tcos, tsin, whi, wlo, perm)
     return out, values
 

time: 173 us -> 170 us (0.983)
  local copies, waits for them, and re-layouts: 4.48 us -> 2.28 us
  Pallas kernels: 165 us -> 163 us
    unnamed x4 -> x2, local copies, waits for them, and re-layouts: 4.48 us -> 2.28 us
where the time goes in v4:
time: 170 us; the launch traced here: 167 us
  Pallas kernels  163 us (96%)
  local copies, waits for them, and re-layouts  2.28 us (1%)
    pallas_call x1, Pallas kernels, hub_program(): pl.pallas_call(hub_kernel, out_shape=(pltpu.VMEM((components, planes, row...  163 us

profile of v4, /device:TPU:8, one launch (start us, length us, event | category | flops | bytes accessed | tf_op | source)
XLA Modules:
  0.0 166.8 jit_solution(571927092738201845)
XLA Ops:
  1.3 163.2 %shard_map.113 = (f32[3,4,128,512]{3,2,1,0:T(8,128)S(1)}, f32[3,2048]{1,0:T(4,128)S(1)}) custom-call(f32[3,2,4,128,512]{4,3,2,1,0:T(8,128)} %spec.1, s32[1]{0:T(128)S(6)} %copy.16.count_ref, s32[2,2048]{1,0:T(2,128)} %cells.1, f32[3,2048]{1,0:T(4,128)} %offs.1, f32[2,4,512]{2,1,0:T(4,128)} %constant.12.clone.rest_0_, f32[2,8,512]{2,1,0:T(8,128)} %constant.13.clone.rest_1_, ...), custom_call_target="tpu_custom_call" | custom-call | tf_op jit(solution)/shard_map/pallas_call | solution.py:588
  164.5 1.7 copy.14
  166.2 0.6 copy.15
